TPU v7x, 256 devices: a whole 4x4x8 slice. The times are simulated.
256 devices in a mesh: seq: 32 (over x, y, core), tensor: 8 (over z).
Axes of the slice: x: 4, y: 4, z: 8, core: 2. Of those that a mesh axis runs over, the one named last changes fastest.
Arguments:
- tokens: bfloat16 [16384, 4096], P('seq', 'tensor'), may hold values from -6 to 6
- norm_gain: float32 [4096], replicated, may hold values from 0.1 to 1.9
- w_query: bfloat16 [4096, 4096], P('seq', 'tensor'), may hold values from -0.09375 to 0.09375
- w_key: bfloat16 [4096, 4096], P('seq', 'tensor'), may hold values from -0.09375 to 0.09375
- w_value: bfloat16 [4096, 4096], P('seq', 'tensor'), may hold values from -0.09375 to 0.09375
- out_gain: float32 [4096], P('tensor'), may hold values from 0.1 to 1.9
- carried: float32 [32, 128, 128], P('tensor'), may hold values from -384 to 384
Outputs:
- attended: bfloat16 [16384, 4096], P('seq', 'tensor')
- final_state: float32 [32, 128, 128], P('tensor')
All inputs are finite; a program needn't handle non-finite values.
Results may differ from a plain program's by a relative error of at most 0.009.
Values may be sent and summed in bfloat16 or wider, within the bound.
No kernel may reach another device: no remote copies, remote signals or barrier semaphores. Data moves between devices by JAX's collectives and lax.ppermute only.
A program may use at most 64 MiB of HBM per device.

v0:
```python
import jax
import jax.numpy as jnp
from jax import lax
from jax.sharding import PartitionSpec as P

BLOCK = 512


def add_rows(normed, pieces):
    return tuple((jnp.dot(normed, piece, preferred_element_type=jnp.float32) for piece in pieces))


def shards(tokens, norm_gain, w_query, w_key, w_value, out_gain, carried):
    whole = lax.all_gather(tokens, "tensor", axis=1, tiled=True)
    xf = whole.astype(jnp.float32)
    normed = (xf * lax.rsqrt(jnp.mean(xf * xf, axis=1, keepdims=True) + 1e-05) * norm_gain).astype(
        jnp.bfloat16
    )
    rows = normed.shape[0]
    width = w_query.shape[1]
    size = carried.shape[1]
    heads = width // size
    qsum, ksum, vsum = add_rows(
        normed,
        (
            lax.all_gather(w_query, "seq", axis=0, tiled=True),
            lax.all_gather(w_key, "seq", axis=0, tiled=True),
            lax.all_gather(w_value, "seq", axis=0, tiled=True),
        ),
    )
    blocks = rows // BLOCK
    query = qsum.astype(jnp.bfloat16).reshape(blocks, BLOCK, heads, size)
    key = ksum.astype(jnp.bfloat16).reshape(blocks, BLOCK, heads, size)
    value = vsum.astype(jnp.bfloat16).reshape(blocks, BLOCK, heads, size)
    block_state = jnp.einsum("nthd,nthe->nhde", key, value, preferred_element_type=jnp.float32)
    local_total = jnp.sum(block_state, axis=0)
    zero_state = jnp.zeros_like(local_total)
    mine = lax.axis_index("seq")
    piece = lax.all_gather(
        local_total[None].astype(jnp.bfloat16), "seq", axis=0, tiled=True
    ).astype(jnp.float32)
    where = jnp.arange(piece.shape[0], dtype=jnp.int32)
    keep = (where < mine).astype(jnp.float32)
    before = zero_state + jnp.sum(keep[:, None, None, None] * piece, axis=0)
    total = zero_state + jnp.sum(piece, axis=0)
    start_state = carried + before
    running = jnp.cumsum(block_state, axis=0) - block_state
    priors = start_state[None] + running
    inter = jnp.einsum(
        "nthd,nhde->nthe", query.astype(jnp.float32), priors, precision=lax.Precision.HIGHEST
    )
    causal = jnp.tril(jnp.ones((BLOCK, BLOCK), jnp.float32))
    scores = jnp.einsum("nthd,nshd->nhts", query, key, preferred_element_type=jnp.float32)
    weights = (scores * causal).astype(jnp.bfloat16)
    intra = jnp.einsum("nhts,nshe->nthe", weights, value, preferred_element_type=jnp.float32)
    raw = inter + intra
    normal = (
        raw
        * lax.rsqrt(jnp.mean(raw * raw, axis=3, keepdims=True) + 1e-06)
        * out_gain.reshape(heads, size)
    )
    attended = normal.astype(jnp.bfloat16).reshape(rows, width)
    return (attended, carried + total)


def solution(mesh):
    return jax.shard_map(
        shards,
        mesh=mesh,
        in_specs=(
            P("seq", "tensor"),
            P(),
            P("seq", "tensor"),
            P("seq", "tensor"),
            P("seq", "tensor"),
            P("tensor"),
            P("tensor", None, None),
        ),
        out_specs=(P("seq", "tensor"), P("tensor", None, None)),
        check_vma=False,
    )
```

profile of v0, /device:TPU:1, one launch (start us, length us, event | category | flops | bytes accessed | tf_op | source)
XLA Modules:
  0.0 293.1 jit_solution(6839959478735101237)
XLA Ops:
  7.2 0.0 copy-start.4
  7.2 0.0 all-gather.7.cloned.1.call-start
  7.2 0.7 all-gather.7.cloned.1.call-update
  7.9 0.0 all-gather.9.cloned.1.call-start
  8.0 0.7 all-gather.9.cloned.1.call-update
  8.7 0.0 all-gather.11.cloned.1.call-start
  8.7 0.7 all-gather.11.cloned.1.call-update
  9.4 0.0 all-gather.13.cloned.1.call-start
  9.4 0.5 all-gather.13.cloned.1.call-update
  10.0 0.0 all-gather.15.cloned.1.call-start
  10.0 58.4 %all-gather.7.cloned.1.call-done = bf16[512,4096]{1,0:T(8,128)(2,1)} async-done(((bf16[512,512]{1,0:T(8,128)(2,1)}), bf16[512,4096]{1,0:T(8,128)(2,1)}) %all-gather.7.cloned.1.call-update) | async-done | bytes 4194320 | tf_op jit(solution)/shard_map/all_gather | solution.py:14
  68.5 3.1 %fusion = f32[512]{0:T(512)S(1)} fusion(bf16[512,4096]{1,0:T(8,128)(2,1)} %all-gather.7.cloned.1.call-done), kind=kLoop, calls=%fused_computation.4 | loop fusion | flops 6290944 | bytes 4196352 | tf_op jit(solution)/shard_map/reduce_sum | solution.py:16
  71.5 49.6 %all-gather.9.cloned.1.call-done = bf16[4096,512]{1,0:T(8,128)(2,1)} async-done(((bf16[128,512]{1,0:T(8,128)(2,1)}), bf16[4096,512]{1,0:T(8,128)(2,1)}) %all-gather.9.cloned.1.call-update) | async-done | bytes 4194320 | tf_op jit(solution)/shard_map/all_gather | solution.py:27
  121.2 0.0 copy-done.4
  121.2 5.9 %convolution_convert_fusion.2 = bf16[512,512]{0,1:T(8,128)(2,1)S(1)} fusion(bf16[4096,512]{1,0:T(8,128)(2,1)} %all-gather.9.cloned.1.call-done, bf16[512,4096]{1,0:T(8,128)(2,1)} %all-gather.7.cloned.1.call-done, f32[4096]{0:T(1024)S(1)} %copy-done.4, f32[512]{0:T(512)S(1)} %add_rsqrt_fusion.1), kind=kOutput, calls=%fused_computation.14 | convolution fusion | flops 2156134400 | bytes 8931328 | tf_op jit(solution)/shard_map/dot_general | solution.py:10
  127.1 47.2 %all-gather.11.cloned.1.call-done = bf16[4096,512]{1,0:T(8,128)(2,1)} async-done(((bf16[128,512]{1,0:T(8,128)(2,1)}), bf16[4096,512]{1,0:T(8,128)(2,1)}) %all-gather.11.cloned.1.call-update) | async-done | bytes 4194320 | tf_op jit(solution)/shard_map/all_gather | solution.py:28
  174.3 5.9 %convolution_convert_fusion.1 = bf16[512,512]{0,1:T(8,128)(2,1)S(1)} fusion(bf16[4096,512]{1,0:T(8,128)(2,1)} %all-gather.11.cloned.1.call-done, bf16[512,4096]{1,0:T(8,128)(2,1)} %all-gather.7.cloned.1.call-done, f32[4096]{0:T(1024)S(1)} %copy-done.4, f32[512]{0:T(512)S(1)} %add_rsqrt_fusion.1), kind=kOutput, calls=%fused_computation.13 | convolution fusion | flops 2156134400 | bytes 8931328 | tf_op jit(solution)/shard_map/dot_general | solution.py:10
  180.2 1.0 fusion.13
  181.3 0.0 all-gather.15.cloned.1.call-update
  181.3 0.1 fusion.6
  181.4 45.8 %all-gather.13.cloned.1.call-done = bf16[4096,512]{1,0:T(8,128)(2,1)} async-done(((bf16[128,512]{1,0:T(8,128)(2,1)}), bf16[4096,512]{1,0:T(8,128)(2,1)}) %all-gather.13.cloned.1.call-update) | async-done | bytes 4194320 | tf_op jit(solution)/shard_map/all_gather | solution.py:26
  227.2 6.7 %convolution_convert_fusion = bf16[512,512]{0,1:T(8,128)(2,1)} fusion(bf16[4096,512]{1,0:T(8,128)(2,1)} %all-gather.13.cloned.1.call-done, bf16[512,4096]{1,0:T(8,128)(2,1)} %all-gather.7.cloned.1.call-done, f32[4096]{0:T(1024)S(1)} %copy-done.4, f32[512]{0:T(512)S(1)} %add_rsqrt_fusion.1), kind=kOutput, calls=%fused_computation.12 | convolution fusion | flops 2156134400 | bytes 8931328 | tf_op jit(solution)/shard_map/dot_general | solution.py:10
  234.0 0.0 copy-start.1
  234.0 2.5 fusion.4
  236.5 0.0 copy-start
  236.5 0.0 copy-start.2
  236.5 0.0 copy-start.3
  236.5 43.7 %all-gather.15.cloned.1.call-done = bf16[128,128,128]{2,1,0:T(8,128)(2,1)} async-done(((bf16[4,128,128]{2,1,0:T(8,128)(2,1)}), bf16[128,128,128]{2,1,0:T(8,128)(2,1)}) %all-gather.15.cloned.1.call-update) | async-done | bytes 4194320 | tf_op jit(solution)/shard_map/all_gather | solution.py:39
  280.2 3.6 %convert_reduce_fusion = (f32[4,128,128]{2,1,0:T(8,128)S(1)}, f32[4,128,128]{2,1,0:T(8,128)S(1)}) fusion(bf16[32,4,128,128]{3,2,1,0:T(8,128)(2,1)} %bitcast.20, f32[32]{0:T(128)S(1)} %compare_convert_fusion), kind=kLoop, calls=%fused_computation | loop fusion | flops 8257536 | bytes 4718720 | tf_op jit(solution)/shard_map/reduce_sum | solution.py:45
  283.8 0.0 copy-done.1
  283.8 0.0 copy-done
  283.9 0.0 copy-done.2
  283.9 0.7 multiply_reduce_fusion
  284.6 0.0 copy-done.3
  284.6 0.2 multiply_convert_fusion.1
  284.8 1.0 copy.16
  285.8 0.7 add.52
  (3 shorter events, 0.0 us)
Async XLA Ops:
  7.2 114.0 %copy-start.4 = (f32[4096]{0:T(1024)S(1)}, f32[4096]{0:T(1024)}, u32[]{:S(2)}) copy-start(f32[4096]{0:T(1024)} %param.8) | copy-start | bytes 49156
  7.2 61.3 %all-gather.7.cloned.1.call-start = ((), (), s32[]{:S(2)}) async-start(), calls=%async_computation | async-start | bytes 4718592 | tf_op jit(solution)/shard_map/all_gather | solution.py:14
  7.9 113.2 %all-gather.9.cloned.1.call-start = ((), (), s32[]{:S(2)}) async-start(), calls=%async_computation.1 | async-start | bytes 4325376 | tf_op jit(solution)/shard_map/all_gather | solution.py:27
  8.7 165.6 %all-gather.11.cloned.1.call-start = ((), (), s32[]{:S(2)}) async-start(), calls=%async_computation.2 | async-start | bytes 4325376 | tf_op jit(solution)/shard_map/all_gather | solution.py:28
  9.4 217.8 %all-gather.13.cloned.1.call-start = ((), (), s32[]{:S(2)}) async-start(), calls=%async_computation.3 | async-start | bytes 4325376 | tf_op jit(solution)/shard_map/all_gather | solution.py:26
  10.0 270.2 %all-gather.15.cloned.1.call-start = ((), (), s32[]{:S(2)}) async-start(), calls=%async_computation.4 | async-start | bytes 4325376 | tf_op jit(solution)/shard_map/all_gather | solution.py:39
  234.0 49.9 %copy-start.1 = (f32[4,128,128]{2,1,0:T(8,128)S(1)}, f32[4,128,128]{2,1,0:T(8,128)}, u32[]{:S(2)}) copy-start(f32[4,128,128]{2,1,0:T(8,128)} %param.13) | copy-start | bytes 786436
  236.5 47.4 %copy-start = (bf16[512,512]{0,1:T(8,128)(2,1)S(1)}, bf16[512,512]{0,1:T(8,128)(2,1)}, u32[]{:S(2)}) copy-start(bf16[512,512]{0,1:T(8,128)(2,1)} %convolution_convert_fusion) | copy-start | bytes 1572868
  236.5 47.4 %copy-start.2 = (f32[4,128,128]{2,1,0:T(8,128)S(1)}, f32[4,128,128]{2,1,0:T(8,128)}, u32[]{:S(2)}) copy-start(f32[4,128,128]{2,1,0:T(8,128)} %get-tuple-element.9) | copy-start | bytes 786436
  236.5 48.1 %copy-start.3 = (f32[512]{0:T(512)S(1)}, f32[512]{0:T(512)}, u32[]{:S(2)}) copy-start(f32[512]{0:T(512)} %param.12) | copy-start | bytes 6148
Sparse Core Ops, SparseCore 0:
  9.8 58.6 all-gather.6
  71.0 50.0 all-gather.8
  123.7 50.5 all-gather.10
  176.7 50.5 all-gather.12
  229.6 50.5 all-gather.14
where the time goes:
time: 293 us
  waiting for transfers between devices  247 us (84%)
  matrix products  22.9 us (8%)
  between operations  13.9 us (5%)
  other arithmetic  7.74 us (3%)
    all_gather x1, waiting for transfers between devices, shards(): whole = lax.all_gather(tokens, 'tensor', axis=1, tiled=True)  58.4 us
    all_gather x1, waiting for transfers between devices, shards(): lax.all_gather(w_key, 'seq', axis=0, tiled=True)  49.6 us
    all_gather x1, waiting for transfers between devices, shards(): lax.all_gather(w_value, 'seq', axis=0, tiled=True)  47.2 us
    all_gather x1, waiting for transfers between devices, shards(): lax.all_gather(w_query, 'seq', axis=0, tiled=True)  45.8 us
    all_gather x1, waiting for transfers between devices, shards(): lax.all_gather(local_total[None].astype(jnp.bfloat16), 'seq', axis=0, til...  43.7 us
    dot_general x3, matrix products, add_rows(): jnp.dot(normed, piece, preferred_element_type=jnp.float32)  18.6 us
  transfers between devices with their start and end apart: 5, of which 5 were waited for; matrix products, arithmetic and copies ran while one was open for 9% of the time, Pallas kernels for 0%

commit v1 on v0

--- a/solution.py
+++ b/solution.py
@@ -11,7 +11,30 @@
 
 
 def shards(tokens, norm_gain, w_query, w_key, w_value, out_gain, carried):
-    whole = lax.all_gather(tokens, "tensor", axis=1, tiled=True)
+    now, d_next, tile_out = (lax.psum(1, "tensor"), lax.axis_index("tensor"), tokens.shape[1])
+    vals = []
+    for s, at in enumerate(tokens.shape):
+        vals.append(at * now if s == 1 else at)
+    whole = lax.dynamic_update_slice_in_dim(
+        jnp.zeros(vals, tokens.dtype), tokens, d_next * tile_out, axis=1
+    )
+    small = step_out = tokens
+    for idx in tuple(range(1, now // 2 + 1)):
+        by_rank = []
+        for s in [*range(now)]:
+            by_rank.append((s, (s + 1) % now))
+        small = lax.ppermute(small, "tensor", by_rank)
+        whole = lax.dynamic_update_slice_in_dim(
+            whole, small, (d_next - idx) % now * tile_out, axis=1
+        )
+        if 2 * idx < now:
+            entries = []
+            for s in tuple(range(now)):
+                entries.append((s, (s - 1) % now))
+            step_out = lax.ppermute(step_out, "tensor", entries)
+            whole = lax.dynamic_update_slice_in_dim(
+                whole, step_out, (d_next + idx) % now * tile_out, axis=1
+            )
     xf = whole.astype(jnp.float32)
     normed = (xf * lax.rsqrt(jnp.mean(xf * xf, axis=1, keepdims=True) + 1e-05) * norm_gain).astype(
         jnp.bfloat16

time: 293 us -> 238 us (0.81)
  waiting for transfers between devices: 247 us -> 179 us
  starting transfers between devices: 0.19 us -> 12.2 us
  local copies, waits for them, and re-layouts: 1.03 us -> 4.02 us
    all_gather x1 -> x0, waiting for transfers between devices: 58.4 us -> none  [shards(): whole = lax.all_gather(tokens, 'tensor', axis=1, tiled=True)]
    all_gather x1, waiting for transfers between devices: 49.6 us -> 0.02 us  [shards(): lax.all_gather(w_key, 'seq', axis=0, tiled=True)]
    ppermute x0 -> x7, waiting for transfers between devices: none -> 42.9 us  [the longest x4 42.9 us: shards(): small = lax.ppermute(small, 'tensor', by_rank)]
    ppermute x0 -> x7, starting transfers between devices: none -> 12 us  [the longest x3 9.45 us: shards(): step_out = lax.ppermute(step_out, 'tensor', entries)]
  transfers between devices with their start and end apart: 5 -> 11, of which waited for: 5 -> 7; matrix products, arithmetic and copies ran while one was open for 9% -> 10% of each run, Pallas kernels for 0% -> 0%
where the time goes in v1:
time: 238 us
  waiting for transfers between devices  179 us (75%)
  matrix products  22.8 us (10%)
  between operations  14 us (6%)
  starting transfers between devices  12.2 us (5%)
  other arithmetic  5.54 us (2%)
  local copies, waits for them, and re-layouts  4.02 us (2%)
    all_gather x1, waiting for transfers between devices, shards(): lax.all_gather(w_query, 'seq', axis=0, tiled=True)  46 us
    all_gather x1, waiting for transfers between devices, shards(): lax.all_gather(w_value, 'seq', axis=0, tiled=True)  44.7 us
    all_gather x1, waiting for transfers between devices, shards(): lax.all_gather(local_total[None].astype(jnp.bfloat16), 'seq', axis=0, til...  43.7 us
    ppermute x4, waiting for transfers between devices, shards(): small = lax.ppermute(small, 'tensor', by_rank)  42.9 us
    dot_general x3, matrix products, add_rows(): jnp.dot(normed, piece, preferred_element_type=jnp.float32)  18.6 us
    ppermute x3, starting transfers between devices, shards(): step_out = lax.ppermute(step_out, 'tensor', entries)  9.45 us
  transfers between devices with their start and end apart: 11, of which 7 were waited for; matrix products, arithmetic and copies ran while one was open for 10% of the time, Pallas kernels for 0%

profile of v1, /device:TPU:1, one launch (start us, length us, event | category | flops | bytes accessed | tf_op | source)
XLA Modules:
  0.0 237.9 jit_solution(14697168734150610838)
XLA Ops:
  7.2 0.0 copy-start.4
  7.2 0.0 all-gather.6.cloned.1.call-start
  7.2 0.7 all-gather.6.cloned.1.call-update
  7.9 0.0 all-gather.8.cloned.1.call-start
  8.0 0.7 all-gather.8.cloned.1.call-update
  8.7 0.0 all-gather.10.cloned.1.call-start
  8.7 0.7 all-gather.10.cloned.1.call-update
  9.4 0.0 all-gather.12.cloned.1.call-start
  9.4 2.5 %collective-permute-start = (bf16[512,512]{1,0:T(8,128)(2,1)}, bf16[512,512]{1,0:T(8,128)(2,1)S(1)}, u32[]{:S(2)}, u32[]{:S(2)}) collective-permute-start(bf16[512,512]{1,0:T(8,128)(2,1)} %param.7), channel_id=1, source_target_pairs={{0,1},{1,2},{2,3},{3,4},{4,5},{5,6},{6,7},{7,0},{8,9},{9,10},{10,1... | collective-permute-start | bytes 1572872 | tf_op jit(solution)/shard_map/ppermute | solution.py:26
  12.0 4.0 %collective-permute-start.1 = (bf16[512,512]{1,0:T(8,128)(2,1)}, bf16[512,512]{1,0:T(8,128)(2,1)S(1)}, u32[]{:S(2)}, u32[]{:S(2)}) collective-permute-start(bf16[512,512]{1,0:T(8,128)(2,1)} %param.7), channel_id=1, source_target_pairs={{0,7},{1,0},{2,1},{3,2},{4,3},{5,4},{6,5},{7,6},{8,15},{9,8},{10,9... | collective-permute-start | bytes 1572872 | tf_op jit(solution)/shard_map/ppermute | solution.py:34
  16.0 11.8 %collective-permute-done = bf16[512,512]{1,0:T(8,128)(2,1)S(1)} collective-permute-done((bf16[512,512]{1,0:T(8,128)(2,1)}, bf16[512,512]{1,0:T(8,128)(2,1)S(1)}, u32[]{:S(2)}, u32[]{:S(2)}) %collective-permute-start) | collective-permute-done | bytes 524320 | tf_op jit(solution)/shard_map/ppermute | solution.py:26
  27.8 0.0 collective-permute-start.2
  27.8 0.0 collective-permute-done.1
  27.8 2.7 %collective-permute-start.3 = (bf16[512,512]{1,0:T(8,128)(2,1)S(1)}, bf16[512,512]{1,0:T(8,128)(2,1)S(1)}, u32[]{:S(2)}, u32[]{:S(2)}) collective-permute-start(bf16[512,512]{1,0:T(8,128)(2,1)S(1)} %collective-permute-done.1), channel_id=1, source_target_pairs={{0,7},{1,0},{2,1},{3,2},{4,3},{5,4},{6,5},{7,6},{8,15},{9,8},{10,9... | collective-permute-start | bytes 1572872 | tf_op jit(solution)/shard_map/ppermute | solution.py:34
  30.5 10.7 %collective-permute-done.2 = bf16[512,512]{1,0:T(8,128)(2,1)S(1)} collective-permute-done((bf16[512,512]{1,0:T(8,128)(2,1)S(1)}, bf16[512,512]{1,0:T(8,128)(2,1)S(1)}, u32[]{:S(2)}, u32[]{:S(2)}) %collective-permute-start.2) | collective-permute-done | bytes 524320 | tf_op jit(solution)/shard_map/ppermute | solution.py:26
  41.2 0.0 collective-permute-start.4
  41.2 0.5 broadcast_in_dim.7
  41.7 0.0 copy-done.4
  41.7 0.1 constant_dynamic-update-slice_fusion.7
  41.8 0.0 collective-permute-done.3
  41.8 2.7 %collective-permute-start.5 = (bf16[512,512]{1,0:T(8,128)(2,1)S(1)}, bf16[512,512]{1,0:T(8,128)(2,1)S(1)}, u32[]{:S(2)}, u32[]{:S(2)}) collective-permute-start(bf16[512,512]{1,0:T(8,128)(2,1)S(1)} %collective-permute-done.3), channel_id=1, source_target_pairs={{0,7},{1,0},{2,1},{3,2},{4,3},{5,4},{6,5},{7,6},{8,15},{9,8},{10,9... | collective-permute-start | bytes 1572872 | tf_op jit(solution)/shard_map/ppermute | solution.py:34
  44.5 0.1 constant_dynamic-update-slice_fusion.6
  44.6 9.2 %collective-permute-done.4 = bf16[512,512]{1,0:T(8,128)(2,1)S(1)} collective-permute-done((bf16[512,512]{1,0:T(8,128)(2,1)S(1)}, bf16[512,512]{1,0:T(8,128)(2,1)S(1)}, u32[]{:S(2)}, u32[]{:S(2)}) %collective-permute-start.4) | collective-permute-done | bytes 524320 | tf_op jit(solution)/shard_map/ppermute | solution.py:26
  53.8 0.0 collective-permute-start.6
  53.8 0.1 constant_dynamic-update-slice_fusion.5
  53.8 0.1 constant_dynamic-update-slice_fusion.4
  53.9 0.0 copy-start.6
  53.9 0.1 constant_dynamic-update-slice_fusion.3
  54.0 0.1 constant_dynamic-update-slice_fusion.2
  54.1 0.0 collective-permute-done.5
  54.1 0.1 constant_dynamic-update-slice_fusion.1
  54.2 11.3 %collective-permute-done.6 = bf16[512,512]{1,0:T(8,128)(2,1)S(1)} collective-permute-done((bf16[512,512]{1,0:T(8,128)(2,1)S(1)}, bf16[512,512]{1,0:T(8,128)(2,1)S(1)}, u32[]{:S(2)}, u32[]{:S(2)}) %collective-permute-start.6) | collective-permute-done | bytes 524320 | tf_op jit(solution)/shard_map/ppermute | solution.py:26
  65.4 0.1 constant_dynamic-update-slice_fusion
  65.5 0.0 copy-start
  65.5 2.0 copy-done
  67.5 0.9 fusion
  68.4 0.0 all-gather.6.cloned.1.call-done
  68.4 0.0 copy-done.6
  68.4 5.9 %convolution_convert_fusion.2 = bf16[512,512]{0,1:T(8,128)(2,1)S(1)} fusion(bf16[4096,512]{1,0:T(8,128)(2,1)} %all-gather.6.cloned.1.call-done, bf16[512,4096]{1,0:T(8,128)(2,1)} %copy-done, f32[4096]{0:T(1024)S(1)} %copy-done.6, f32[512]{0:T(512)S(1)} %add_rsqrt_fusion.1), kind=kOutput, calls=%fused_computation.14 | convolution fusion | flops 2156134400 | bytes 8931328 | tf_op jit(solution)/shard_map/dot_general | solution.py:10
  74.3 44.7 %all-gather.8.cloned.1.call-done = bf16[4096,512]{1,0:T(8,128)(2,1)} async-done(((bf16[128,512]{1,0:T(8,128)(2,1)}), bf16[4096,512]{1,0:T(8,128)(2,1)}) %all-gather.8.cloned.1.call-update) | async-done | bytes 4194320 | tf_op jit(solution)/shard_map/all_gather | solution.py:51
  119.0 5.9 %convolution_convert_fusion.1 = bf16[512,512]{0,1:T(8,128)(2,1)S(1)} fusion(bf16[4096,512]{1,0:T(8,128)(2,1)} %all-gather.8.cloned.1.call-done, bf16[512,4096]{1,0:T(8,128)(2,1)} %copy-done, f32[4096]{0:T(1024)S(1)} %copy-done.6, f32[512]{0:T(512)S(1)} %add_rsqrt_fusion.1), kind=kOutput, calls=%fused_computation.13 | convolution fusion | flops 2156134400 | bytes 8931328 | tf_op jit(solution)/shard_map/dot_general | solution.py:10
  124.9 1.0 fusion.13
  126.0 0.0 all-gather.12.cloned.1.call-update
  126.0 0.1 fusion.6
  126.1 46.0 %all-gather.10.cloned.1.call-done = bf16[4096,512]{1,0:T(8,128)(2,1)} async-done(((bf16[128,512]{1,0:T(8,128)(2,1)}), bf16[4096,512]{1,0:T(8,128)(2,1)}) %all-gather.10.cloned.1.call-update) | async-done | bytes 4194320 | tf_op jit(solution)/shard_map/all_gather | solution.py:49
  172.1 6.7 %convolution_convert_fusion = bf16[512,512]{0,1:T(8,128)(2,1)} fusion(bf16[4096,512]{1,0:T(8,128)(2,1)} %all-gather.10.cloned.1.call-done, bf16[512,4096]{1,0:T(8,128)(2,1)} %copy-done, f32[4096]{0:T(1024)S(1)} %copy-done.6, f32[512]{0:T(512)S(1)} %add_rsqrt_fusion.1), kind=kOutput, calls=%fused_computation.12 | convolution fusion | flops 2156134400 | bytes 8931328 | tf_op jit(solution)/shard_map/dot_general | solution.py:10
  178.8 0.0 copy-start.2
  178.8 2.5 %fusion.4 = f32[4,128,512]{2,1,0:T(8,128)S(1)} fusion(bf16[512,4,128]{0,2,1:T(8,128)(2,1)S(1)} %bitcast.24, bf16[512,4,128]{0,2,1:T(8,128)(2,1)} %bitcast.25, bf16[512,4,128]{0,2,1:T(8,128)(2,1)S(1)} %bitcast.22, f32[512,512]{1,0:T(8,128)S(1)} %fusion.6), kind=kOutput, calls=%fused_computation.9 | convolution fusion | flops 538968064 | bytes 3670016 | tf_op jit(solution)/shard_map/nhts,nshe->nthe/dot_general | solution.py:78
  181.3 0.0 copy-start.1
  181.3 0.0 copy-start.3
  181.3 0.0 copy-start.5
  181.4 43.7 %all-gather.12.cloned.1.call-done = bf16[128,128,128]{2,1,0:T(8,128)(2,1)} async-done(((bf16[4,128,128]{2,1,0:T(8,128)(2,1)}), bf16[128,128,128]{2,1,0:T(8,128)(2,1)}) %all-gather.12.cloned.1.call-update) | async-done | bytes 4194320 | tf_op jit(solution)/shard_map/all_gather | solution.py:62
  225.1 3.6 %convert_reduce_fusion = (f32[4,128,128]{2,1,0:T(8,128)S(1)}, f32[4,128,128]{2,1,0:T(8,128)S(1)}) fusion(bf16[32,4,128,128]{3,2,1,0:T(8,128)(2,1)} %bitcast.20, f32[32]{0:T(128)S(1)} %compare_convert_fusion), kind=kLoop, calls=%fused_computation | loop fusion | flops 8257536 | bytes 4718720 | tf_op jit(solution)/shard_map/reduce_sum | solution.py:68
  228.7 0.0 copy-done.2
  228.7 0.0 copy-done.1
  228.7 0.0 copy-done.3
  228.8 0.7 multiply_reduce_fusion
  229.5 0.0 copy-done.5
  229.5 0.2 multiply_convert_fusion.1
  229.6 1.0 copy.16
  230.7 0.7 add.129
  (3 shorter events, 0.0 us)
Async XLA Ops:
  7.2 34.5 %copy-start.4 = (bf16[512,512]{1,0:T(8,128)(2,1)S(1)}, bf16[512,512]{1,0:T(8,128)(2,1)}, u32[]{:S(2)}) copy-start(bf16[512,512]{1,0:T(8,128)(2,1)} %param.7) | copy-start | bytes 1572868
  7.2 61.2 %all-gather.6.cloned.1.call-start = ((), (), s32[]{:S(2)}) async-start(), calls=%async_computation | async-start | bytes 4325376 | tf_op jit(solution)/shard_map/all_gather | solution.py:50
  7.9 111.1 %all-gather.8.cloned.1.call-start = ((), (), s32[]{:S(2)}) async-start(), calls=%async_computation.1 | async-start | bytes 4325376 | tf_op jit(solution)/shard_map/all_gather | solution.py:51
  8.7 163.5 %all-gather.10.cloned.1.call-start = ((), (), s32[]{:S(2)}) async-start(), calls=%async_computation.2 | async-start | bytes 4325376 | tf_op jit(solution)/shard_map/all_gather | solution.py:49
  9.4 215.7 %all-gather.12.cloned.1.call-start = ((), (), s32[]{:S(2)}) async-start(), calls=%async_computation.3 | async-start | bytes 4325376 | tf_op jit(solution)/shard_map/all_gather | solution.py:62
  9.4 18.3 %collective-permute-start = (bf16[512,512]{1,0:T(8,128)(2,1)}, bf16[512,512]{1,0:T(8,128)(2,1)S(1)}, u32[]{:S(2)}, u32[]{:S(2)}) collective-permute-start(bf16[512,512]{1,0:T(8,128)(2,1)} %param.7), channel_id=1, source_target_pairs={{0,1},{1,2},{2,3},{3,4},{4,5},{5,6},{6,7},{7,0},{8,9},{9,10},{10,1... | collective-permute-start | bytes 1572872 | tf_op jit(solution)/shard_map/ppermute | solution.py:26
  12.0 15.8 %collective-permute-start.1 = (bf16[512,512]{1,0:T(8,128)(2,1)}, bf16[512,512]{1,0:T(8,128)(2,1)S(1)}, u32[]{:S(2)}, u32[]{:S(2)}) collective-permute-start(bf16[512,512]{1,0:T(8,128)(2,1)} %param.7), channel_id=1, source_target_pairs={{0,7},{1,0},{2,1},{3,2},{4,3},{5,4},{6,5},{7,6},{8,15},{9,8},{10,9... | collective-permute-start | bytes 1572872 | tf_op jit(solution)/shard_map/ppermute | solution.py:34
  27.8 13.4 %collective-permute-start.2 = (bf16[512,512]{1,0:T(8,128)(2,1)S(1)}, bf16[512,512]{1,0:T(8,128)(2,1)S(1)}, u32[]{:S(2)}, u32[]{:S(2)}) collective-permute-start(bf16[512,512]{1,0:T(8,128)(2,1)S(1)} %collective-permute-done), channel_id=1, source_target_pairs={{0,1},{1,2},{2,3},{3,4},{4,5},{5,6},{6,7},{7,0},{8,9},{9,10},{10,1... | collective-permute-start | bytes 1572872 | tf_op jit(solution)/shard_map/ppermute | solution.py:26
  27.8 14.0 %collective-permute-start.3 = (bf16[512,512]{1,0:T(8,128)(2,1)S(1)}, bf16[512,512]{1,0:T(8,128)(2,1)S(1)}, u32[]{:S(2)}, u32[]{:S(2)}) collective-permute-start(bf16[512,512]{1,0:T(8,128)(2,1)S(1)} %collective-permute-done.1), channel_id=1, source_target_pairs={{0,7},{1,0},{2,1},{3,2},{4,3},{5,4},{6,5},{7,6},{8,15},{9,8},{10,9... | collective-permute-start | bytes 1572872 | tf_op jit(solution)/shard_map/ppermute | solution.py:34
  41.2 12.6 %collective-permute-start.4 = (bf16[512,512]{1,0:T(8,128)(2,1)S(1)}, bf16[512,512]{1,0:T(8,128)(2,1)S(1)}, u32[]{:S(2)}, u32[]{:S(2)}) collective-permute-start(bf16[512,512]{1,0:T(8,128)(2,1)S(1)} %collective-permute-done.2), channel_id=1, source_target_pairs={{0,1},{1,2},{2,3},{3,4},{4,5},{5,6},{6,7},{7,0},{8,9},{9,10},{10,1... | collective-permute-start | bytes 1572872 | tf_op jit(solution)/shard_map/ppermute | solution.py:26
  41.8 12.3 %collective-permute-start.5 = (bf16[512,512]{1,0:T(8,128)(2,1)S(1)}, bf16[512,512]{1,0:T(8,128)(2,1)S(1)}, u32[]{:S(2)}, u32[]{:S(2)}) collective-permute-start(bf16[512,512]{1,0:T(8,128)(2,1)S(1)} %collective-permute-done.3), channel_id=1, source_target_pairs={{0,7},{1,0},{2,1},{3,2},{4,3},{5,4},{6,5},{7,6},{8,15},{9,8},{10,9... | collective-permute-start | bytes 1572872 | tf_op jit(solution)/shard_map/ppermute | solution.py:34
  53.8 11.7 %collective-permute-start.6 = (bf16[512,512]{1,0:T(8,128)(2,1)S(1)}, bf16[512,512]{1,0:T(8,128)(2,1)S(1)}, u32[]{:S(2)}, u32[]{:S(2)}) collective-permute-start(bf16[512,512]{1,0:T(8,128)(2,1)S(1)} %collective-permute-done.4), channel_id=1, source_target_pairs={{0,1},{1,2},{2,3},{3,4},{4,5},{5,6},{6,7},{7,0},{8,9},{9,10},{10,1... | collective-permute-start | bytes 1572872 | tf_op jit(solution)/shard_map/ppermute | solution.py:26
  53.9 14.5 %copy-start.6 = (f32[4096]{0:T(1024)S(1)}, f32[4096]{0:T(1024)}, u32[]{:S(2)}) copy-start(f32[4096]{0:T(1024)} %param.8) | copy-start | bytes 49156
  65.5 2.0 copy-start
  178.8 49.9 %copy-start.2 = (f32[4,128,128]{2,1,0:T(8,128)S(1)}, f32[4,128,128]{2,1,0:T(8,128)}, u32[]{:S(2)}) copy-start(f32[4,128,128]{2,1,0:T(8,128)} %param.13) | copy-start | bytes 786436
  181.3 47.4 %copy-start.1 = (bf16[512,512]{0,1:T(8,128)(2,1)S(1)}, bf16[512,512]{0,1:T(8,128)(2,1)}, u32[]{:S(2)}) copy-start(bf16[512,512]{0,1:T(8,128)(2,1)} %convolution_convert_fusion) | copy-start | bytes 1572868
  181.3 47.4 %copy-start.3 = (f32[4,128,128]{2,1,0:T(8,128)S(1)}, f32[4,128,128]{2,1,0:T(8,128)}, u32[]{:S(2)}) copy-start(f32[4,128,128]{2,1,0:T(8,128)} %get-tuple-element.9) | copy-start | bytes 786436
  181.3 48.1 %copy-start.5 = (f32[512]{0:T(512)S(1)}, f32[512]{0:T(512)}, u32[]{:S(2)}) copy-start(f32[512]{0:T(512)} %param.12) | copy-start | bytes 6148
Sparse Core Ops, SparseCore 0:
  10.6 55.2 all-gather.5
  68.5 50.5 all-gather.7
  121.6 50.5 all-gather.9
  174.5 50.5 all-gather.11
